TPU v7x, 32 devices: a whole 2x2x4 slice. The times are simulated.
32 devices in a mesh: cell: 8 (over z, x), lev: 4 (over y, core).
Axes of the slice: x: 2, y: 2, z: 4, core: 2. Of those that a mesh axis runs over, the one named last changes fastest.
Arguments:
- populations: float32 [512, 8192], P('cell', 'lev'), may hold values from 0.5 to 1.5
- rate_blocks: bfloat16 [2, 64, 6, 128, 128], P(None, 'lev'), may hold values from -0.21875 to 0.21875
- pattern: int32 [64, 6], P('lev'), may hold values from 0 to 63, as said below
- bracket: int32 [512], P('cell'), may hold values from 0 to 1
- cross_section: float32 [8192], P('lev'), as said below
- emission: float32 [8192], P('lev'), may hold values from 0.1 to 1
- absorber: float32 [512], P('cell'), as said below
- stream_speed: float32 [512], P('cell'), may hold values from 0.25 to 1
- cross_speed: float32 [512], P('cell'), may hold values from -1 to 1
- inflow: float32 [16, 8192], P(None, 'lev'), may hold values from 0.5 to 1.5
Outputs:
- updated: float32 [512, 8192], P('cell', 'lev')
- absorption: float32 [512, 8192], P('cell', 'lev')
Inputs may be any that keep to these rules, and one draw needn't show every extreme that they name: Row r of pattern lists 6 distinct level blocks, the first of them r itself. `cross_section`: each cross section lies between 0.1 / 32 and 0.035. `absorber`: absorber columns lie between 0.5 and 2, except a few whole streamwise rows where they equal 48.
All inputs are finite; a program needn't handle non-finite values.
Results may differ from a plain program's by a relative error of at most 0.00055.
Values may be sent and summed in bfloat16 or wider, within the bound.
A program may use at most 128 MiB of HBM per device.

v0:
```python
import functools

import jax
import jax.numpy as jnp
from jax import lax
from jax.experimental import pallas as pl
from jax.experimental.pallas import tpu as pltpu
from jax.sharding import PartitionSpec as P

NY = 16
LANES = 128

time_step = 0.25

MESH = pl.DeviceIdType.MESH


def fused_kernel(
    strips,
    groups,
    pattern_hbm,
    p_hbm,
    rates_hbm,
    bracket_hbm,
    absorber_hbm,
    stream_hbm,
    turn_hbm,
    cross_hbm,
    emission_hbm,
    inflow_hbm,
    advanced_ref,
    gained_ref,
    pattern_ref,
    p_ref,
    bracket_ref,
    absorber_ref,
    stream_ref,
    turn_ref,
    cross_ref,
    emission_ref,
    inflow_ref,
    rates,
    coef,
    passing,
    middle,
    rate_sum,
    gathered_first,
    gathered_second,
    halo,
    columns,
    share_pass,
    out_one,
    in_one,
    out_two,
    in_two,
    rates_sem,
    operand_sem,
    gather_send,
    gather_recv,
    forward_send,
    halo_send,
    halo_recv,
    column_send,
    column_recv,
    one_send,
    one_recv,
    two_send,
    two_recv,
):
    cell = lax.axis_index("cell")
    gathered = (gathered_first, gathered_second)
    lev = lax.axis_index("lev")
    cell_count = p_ref.shape[0]
    layers = cell_count // NY
    blocks = p_ref.shape[1] // LANES
    per_owner = blocks // strips
    brackets, _, nonzero = rates_hbm.shape[:3]
    partner = lev + 1 - 2 * lax.rem(lev, 2)

    operands = [
        pltpu.make_async_copy(source, into, operand_sem.at[index])
        for index, (source, into) in enumerate(
            (
                (p_hbm, p_ref),
                (absorber_hbm, absorber_ref),
                (cross_hbm, cross_ref),
                (emission_hbm, emission_ref),
                (stream_hbm, stream_ref),
                (turn_hbm, turn_ref),
                (bracket_hbm, bracket_ref),
                (inflow_hbm, inflow_ref),
                (pattern_hbm, pattern_ref),
            )
        )
    ]
    for copy in operands:
        copy.start()
    fetch = pltpu.make_async_copy(rates_hbm, rates, rates_sem)
    fetch.start()

    barrier = pltpu.get_barrier_semaphore()
    greeted = 0
    for step in range(1, strips):
        pl.semaphore_signal(
            barrier,
            inc=1,
            device_id={"cell": lax.rem(cell + step, strips), "lev": lev},
            device_id_type=MESH,
        )
        greeted += 1
    for step in range(1, groups // 2):
        pl.semaphore_signal(
            barrier,
            inc=1,
            device_id={"cell": cell, "lev": lax.rem(lev + 2 * step, groups)},
            device_id_type=MESH,
        )
        greeted += 1
    pl.semaphore_signal(barrier, inc=1, device_id={"cell": cell, "lev": partner}, device_id_type=MESH)
    greeted += 1

    def rows(x):
        return slice(x * NY, (x + 1) * NY)

    def spread(row):
        shape = (cell_count, cell_count)
        here = lax.broadcasted_iota(jnp.int32, shape, 0) == lax.broadcasted_iota(jnp.int32, shape, 1)
        column = jnp.sum(jnp.where(here, row, 0.0), axis=1, keepdims=True)
        return jnp.broadcast_to(column, (cell_count, LANES))

    def summed_layers(row):
        shape = (NY, cell_count)
        cell_y = lax.rem(lax.broadcasted_iota(jnp.int32, shape, 1), NY)
        here = lax.broadcasted_iota(jnp.int32, shape, 0) == cell_y
        column = jnp.sum(jnp.where(here, row, 0.0), axis=1, keepdims=True)
        return jnp.broadcast_to(column, (NY, LANES))

    def lanes(block):
        return pl.ds(pl.multiple_of(block * LANES, LANES), LANES)

    chunks = gather_recv.shape[2]
    piece = blocks // chunks

    def own_slot(part, who, chunk):
        return gathered[part].at[pl.ds(who * blocks + chunk * piece, piece)]

    def gather_copy(part, to, source, send_sem, chunk):
        return pltpu.make_async_remote_copy(
            src_ref=own_slot(part, source, chunk),
            dst_ref=own_slot(part, source, chunk),
            send_sem=send_sem.at[chunk],
            recv_sem=gather_recv.at[part, source, chunk],
            device_id={"cell": cell, "lev": to},
            device_id_type=MESH,
        )

    def halo_copy(part):
        return pltpu.make_async_remote_copy(
            src_ref=gathered[part].at[pl.ds(lev * blocks, blocks), pl.ds(cell_count - NY, NY)],
            dst_ref=halo.at[part],
            send_sem=halo_send.at[part],
            recv_sem=halo_recv.at[part],
            device_id={"cell": lax.rem(cell + 1, strips), "lev": lev},
            device_id_type=MESH,
        )

    def column_copy(step):
        to = lax.rem(cell + step, strips)
        return pltpu.make_async_remote_copy(
            src_ref=columns.at[cell],
            dst_ref=columns.at[cell],
            send_sem=column_send.at[step],
            recv_sem=column_recv.at[step],
            device_id={"cell": to, "lev": lev},
            device_id_type=MESH,
        )

    def strip_copy(part, step, out, into, send_sem, recv_sem):
        to = lax.rem(cell + step, strips)
        return pltpu.make_async_remote_copy(
            src_ref=out.at[part, to],
            dst_ref=into.at[part, cell],
            send_sem=send_sem.at[part, step],
            recv_sem=recv_sem.at[part, step],
            device_id={"cell": to, "lev": lev},
            device_id_type=MESH,
        )

    def emitted_of(value, block):
        return value * emission_ref[pl.ds(block, 1), :]

    def put(ref, part, index, downs, ups):
        means = []
        for place, value in enumerate(downs + ups):
            mean = jnp.mean(value, axis=0, keepdims=True).astype(jnp.bfloat16).astype(jnp.float32)
            ref[part, index, place] = (value - mean).astype(jnp.bfloat16)
            means.append(mean)
        means.append(jnp.zeros((NY - len(means), LANES), jnp.float32))
        ref[part, index, 2 * per_owner] = jnp.concatenate(means, axis=0).astype(jnp.bfloat16)

    def get(ref, part, index, b):
        means = ref[part, index, 2 * per_owner].astype(jnp.float32)
        return tuple(
            ref[part, index, place].astype(jnp.float32) + means[place : place + 1]
            for place in (b, per_owner + b)
        )

    def lower(part, block, value):
        gathered[part][lev * blocks + block] = value.astype(jnp.bfloat16)

    def summarize(part, owner, values):
        downs, ups = [], []
        for b in range(per_owner):
            block = owner * per_owner + b
            through = [passing[block, rows(x), :] for x in range(layers)]
            emit = [emitted_of(values[b][x], block) for x in range(layers)]
            down, up = emit[0], emit[-1]
            for x in range(1, layers):
                down = through[x] * down + emit[x]
                up = through[layers - 1 - x] * up + emit[layers - 1 - x]
            downs.append(down)
            ups.append(up)
        put(out_one, part, owner, downs, ups)

    def load_start(block):
        return [p_ref[rows(x), lanes(block)] for x in range(layers)]

    def start_gather(part, chunk):
        for step in range(1, groups // 2):
            to = lax.rem(lev + 2 * step, groups)
            gather_copy(part, to, lev, gather_send.at[part, step], chunk).start()
        gather_copy(part, partner, lev, gather_send.at[part, 0], chunk).start()

    def start_halo(part):
        @pl.when(cell < strips - 1)
        def _():
            halo_copy(part).start()

    def lower_start(block, _):
        lower(0, block, p_ref[:, lanes(block)])
        return 0

    operands[0].wait()
    operands[1].wait()
    columns[cell] = absorber_ref[...]
    pl.semaphore_wait(barrier, greeted)
    for chunk in range(chunks):
        lax.fori_loop(chunk * piece, (chunk + 1) * piece, lower_start, 0, unroll=2)
        start_gather(0, chunk)
    for step in range(1, strips):
        column_copy(step).start()

    for copy in operands[2:]:
        copy.wait()
    coef[0] = spread(absorber_ref[...])

    def pass_block(block, _):
        passing[block] = jnp.exp(-(coef[0] * cross_ref[pl.ds(block, 1), :]))
        return 0

    def summarize_start(owner, _):
        values = []
        for b in range(per_owner):
            pass_block(owner * per_owner + b, 0)
            values.append(load_start(owner * per_owner + b))
        summarize(0, owner, values)
        return 0

    lax.fori_loop(0, strips, summarize_start, 0)

    def start_one(part):
        for step in range(1, strips):
            strip_copy(part, step, out_one, in_one, one_send, one_recv).start()
        in_one[part, cell] = out_one[part, cell]

    start_one(0)
    start_halo(0)
    coef[1] = spread(stream_ref[...])
    coef[2] = spread(turn_ref[...])
    coef[3] = spread(bracket_ref[...].astype(jnp.float32))
    for step in range(1, strips):
        column_copy(step).wait()

    def share_block(strip, _):
        column = summed_layers(columns[strip])
        for b in range(per_owner):
            cross = cross_ref[pl.ds(cell * per_owner + b, 1), :]
            share_pass[strip, b] = jnp.exp(-(column * cross))
        return 0

    lax.fori_loop(0, strips, share_block, 0)

    def enter(part):
        for step in range(1, strips):
            strip_copy(part, step, out_one, in_one, one_send, one_recv).wait()
        below = [[] for _ in range(strips)]
        above = [[] for _ in range(strips)]
        for b in range(per_owner):
            parts = [get(in_one, part, strip, b) for strip in range(strips)]
            running = jnp.zeros((NY, LANES), jnp.float32)
            for strip in range(strips):
                below[strip].append(running)
                running = share_pass[strip, b] * running + parts[strip][0]
            running = jnp.zeros((NY, LANES), jnp.float32)
            for strip in reversed(range(strips)):
                above[strip].append(running)
                running = share_pass[strip, b] * running + parts[strip][1]
        for strip in range(strips):
            put(out_two, part, strip, below[strip], above[strip])
        for step in range(1, strips):
            strip_copy(part, step, out_two, in_two, two_send, two_recv).start()
        in_two[part, cell] = out_two[part, cell]

    def forward(part, chunk):
        for step in range(1, groups // 2):
            source = lax.rem(lev + 2 * step, groups)
            gather_copy(part, lev, source, gather_send.at[part, step], chunk).wait_recv()
            gather_copy(part, partner, source, forward_send.at[part, step], chunk).start()

    def rates_of(part):
        for chunk in range(chunks):
            gather_copy(part, partner, partner, gather_send.at[part, 0], chunk).wait_recv()
            for step in range(1, groups // 2):
                source = lax.rem(partner + 2 * step, groups)
                gather_copy(part, lev, source, gather_send.at[part, step], chunk).wait_recv()

        def one_row(row, _):
            picked = jnp.concatenate(
                [gathered[part][pattern_ref[k, row]] for k in range(nonzero)], axis=1
            )
            table = jnp.concatenate(
                [
                    jnp.concatenate([rates[bracket, row, k] for k in range(nonzero)], axis=1)
                    for bracket in range(brackets)
                ],
                axis=0,
            )
            product = lax.dot_general(
                picked, table, (((1,), (1,)), ((), ())), preferred_element_type=jnp.float32
            )
            kind = coef[3]
            summed = product[:, :LANES]
            for bracket in range(1, brackets):
                summed = jnp.where(
                    kind == float(bracket),
                    product[:, bracket * LANES : (bracket + 1) * LANES],
                    summed,
                )
            rate_sum[row] = summed
            return 0

        lax.fori_loop(0, blocks, one_row, 0, unroll=4)

    def finish_transfers(part):
        for chunk in range(chunks):
            for step in range(1, groups // 2):
                gather_copy(part, partner, lev, gather_send.at[part, step], chunk).wait_send()
                gather_copy(part, partner, lev, forward_send.at[part, step], chunk).wait_send()
            gather_copy(part, partner, lev, gather_send.at[part, 0], chunk).wait_send()

        @pl.when(cell < strips - 1)
        def _():
            halo_copy(part).wait_send()

    def before_close(part):
        @pl.when(cell > 0)
        def _():
            halo_copy(part).wait_recv()

        @pl.when(cell == 0)
        def _():
            for block in range(blocks):
                halo[part, block] = inflow_ref[:, block * LANES : (block + 1) * LANES].astype(
                    jnp.bfloat16
                )

        for step in range(1, strips):
            strip_copy(part, step, out_two, in_two, two_send, two_recv).wait()

    def tendency(part, owner, b, value):
        block = owner * per_owner + b
        through = [passing[block, rows(x), :] for x in range(layers)]
        emit = [emitted_of(value[x], block) for x in range(layers)]
        down, up = get(in_two, part, owner, b)
        downs, ups = [None] * layers, [None] * layers
        for x in range(layers):
            down = through[x] * down + emit[x]
            downs[x] = down
            back = layers - 1 - x
            up = through[back] * up + emit[back]
            ups[back] = up
        arrived = halo[part, block].astype(jnp.float32)
        entering = jnp.where(cell == 0, inflow_ref[:, lanes(block)], arrived)
        gains, total = [], []
        for x in range(layers):
            gained = downs[x] + ups[x] - 2.0 * emit[x]
            taken = (1.0 - through[x]) * gained
            upstream = entering if x == 0 else value[x - 1]
            before_y = pltpu.roll(value[x], 1, 0)
            after_y = pltpu.roll(value[x], NY - 1, 0)
            cross = coef[2, rows(x), :]
            carried = (
                -coef[1, rows(x), :] * (value[x] - upstream)
                - jnp.maximum(cross, 0.0) * (value[x] - before_y)
                - jnp.minimum(cross, 0.0) * (after_y - value[x])
            )
            gains.append(gained)
            total.append(rate_sum[block, rows(x), :] - emit[x] + taken + carried)
        return gains, total

    def exchange(part):
        for chunk in range(chunks - 1):
            forward(part, chunk)
        enter(part)
        forward(part, chunks - 1)

    exchange(0)
    fetch.wait()
    rates_of(0)
    before_close(0)

    def close_first(owner, _):
        values = []
        for b in range(per_owner):
            block = owner * per_owner + b
            value = load_start(block)
            _, total = tendency(0, owner, b, value)
            renewed = [value[x] + time_step * total[x] for x in range(layers)]
            for x in range(layers):
                middle[block, rows(x), :] = renewed[x]
            lower(1, block, jnp.concatenate(renewed, axis=0))
            values.append(renewed)
        summarize(1, owner, values)
        return 0

    owners = strips // chunks
    for chunk in range(chunks):
        lax.fori_loop(chunk * owners, (chunk + 1) * owners, close_first, 0)
        start_gather(1, chunk)
    start_one(1)
    start_halo(1)
    finish_transfers(0)
    exchange(1)
    rates_of(1)
    before_close(1)

    def close_second(owner, _):
        for b in range(per_owner):
            block = owner * per_owner + b
            value = [middle[block, rows(x), :] for x in range(layers)]
            gains, total = tendency(1, owner, b, value)
            for x in range(layers):
                gained_ref[rows(x), lanes(block)] = gains[x]
                advanced_ref[rows(x), lanes(block)] = value[x] + time_step * total[x]
        return 0

    lax.fori_loop(0, strips, close_second, 0)
    finish_transfers(1)


def fused(
    strips,
    groups,
    populations,
    rate_blocks,
    pattern,
    bracket,
    cross_section,
    emission,
    absorber,
    stream_speed,
    cross_speed,
    inflow,
):
    cell_count, level_count = populations.shape
    blocks = level_count // LANES
    per_owner = blocks // strips
    chunks = 4 if strips % 4 == 0 else 1
    layers_shape = (blocks, cell_count, LANES)
    share = (2, strips, 2 * per_owner + 1, NY, LANES)
    vmem = pl.BlockSpec(memory_space=pltpu.VMEM)
    dma = pltpu.SemaphoreType.DMA
    operands = [
        pattern.T,
        populations,
        rate_blocks,
        bracket.reshape(1, -1),
        absorber.reshape(1, -1),
        stream_speed.reshape(1, -1),
        cross_speed.reshape(1, -1),
        cross_section.reshape(blocks, LANES),
        emission.reshape(blocks, LANES),
        inflow,
    ]
    held = [pltpu.VMEM(value.shape, value.dtype) for value in operands]
    held[0] = pltpu.SMEM(operands[0].shape, operands[0].dtype)
    del held[2]
    return pl.pallas_call(
        functools.partial(fused_kernel, strips, groups),
        out_shape=[jax.ShapeDtypeStruct((cell_count, level_count), jnp.float32)] * 2,
        in_specs=[pl.BlockSpec(memory_space=pltpu.HBM)] * len(operands),
        out_specs=[vmem, vmem],
        scratch_shapes=held
        + [
            pltpu.VMEM(rate_blocks.shape, rate_blocks.dtype),
            pltpu.VMEM((4, cell_count, LANES), jnp.float32),
            pltpu.VMEM(layers_shape, jnp.float32),
            pltpu.VMEM(layers_shape, jnp.float32),
            pltpu.VMEM(layers_shape, jnp.float32),
            pltpu.VMEM((groups * blocks, cell_count, LANES), jnp.bfloat16),
            pltpu.VMEM((groups * blocks, cell_count, LANES), jnp.bfloat16),
            pltpu.VMEM((2, blocks, NY, LANES), jnp.bfloat16),
            pltpu.VMEM((strips, 1, cell_count), jnp.float32),
            pltpu.VMEM((strips, per_owner, NY, LANES), jnp.float32),
            pltpu.VMEM(share, jnp.bfloat16),
            pltpu.VMEM(share, jnp.bfloat16),
            pltpu.VMEM(share, jnp.bfloat16),
            pltpu.VMEM(share, jnp.bfloat16),
            dma(()),
            dma((len(held),)),
            dma((2, groups, chunks)),
            dma((2, groups, chunks)),
            dma((2, groups, chunks)),
            dma((2,)),
            dma((2,)),
            dma((strips,)),
            dma((strips,)),
            dma((2, strips)),
            dma((2, strips)),
            dma((2, strips)),
            dma((2, strips)),
        ],
        compiler_params=pltpu.CompilerParams(
            collective_id=0, has_side_effects=True, vmem_limit_bytes=67043328
        ),
    )(*operands)


def shortened(value):

    def short(part):
        return part.astype(jnp.bfloat16) if part.dtype == jnp.float32 else part

    return jax.tree.map(short, value)


def shifted(value, axis, by):
    peers = lax.axis_size(axis)
    pairs = [(i, i + by) for i in range(peers) if 0 <= i + by < peers]
    return lax.ppermute(value, axis, pairs)


def affine(earlier, later):
    return (earlier[0] * later[0], later[0] * earlier[1] + later[1])


def rate_term(populations, rate_blocks, pattern, bracket):
    lowered = populations.astype(jnp.bfloat16)
    gathered = lax.all_gather(lowered, "lev", axis=1, tiled=True)
    cell_count = gathered.shape[0]
    block_size = rate_blocks.shape[3]
    picked = gathered.reshape(cell_count, -1, block_size)[:, pattern, :]
    summed = jnp.zeros((cell_count, rate_blocks.shape[1], block_size), jnp.float32)
    for bracket_id in range(rate_blocks.shape[0]):
        product = jnp.einsum(
            "crkj,rkij->cri", picked, rate_blocks[bracket_id], preferred_element_type=jnp.float32
        )
        summed = jnp.where((bracket == bracket_id)[:, None, None], product, summed)
    return summed.reshape(cell_count, -1)


def entering(received):
    start = jnp.zeros(received.shape[2:], jnp.float32)

    def advance(running, layer_in):
        return (layer_in[0] * running + layer_in[1], running)

    _, from_below = lax.scan(advance, start, (received[:, 0], received[:, 1]))
    _, from_above = lax.scan(advance, start, (received[:, 2], received[:, 3]), reverse=True)
    both_sides = jnp.stack([from_below, from_above], axis=1)
    return lax.all_to_all(both_sides, "cell", split_axis=0, concat_axis=3, tiled=True)


def radiation(populations, emission, cross_section, absorber):
    cell_count, level_count = populations.shape
    strips = cell_count // NY
    emitted = populations * emission[None, :]
    transmit = jnp.exp(-(absorber[:, None] * cross_section[None, :]))
    layered_pass = transmit.reshape(strips, NY, level_count)
    layered_emit = emitted.reshape(strips, NY, level_count)
    passed_down, local_down = lax.associative_scan(affine, (layered_pass, layered_emit), axis=0)
    passed_up, local_up = lax.associative_scan(
        affine, (layered_pass, layered_emit), reverse=True, axis=0
    )
    summary = jnp.stack([passed_down[-1], local_down[-1], passed_up[0], local_up[0]])[None]
    returned = entering(lax.all_to_all(summary, "cell", split_axis=3, concat_axis=0, tiled=True))
    enter_down = returned[0, 0]
    enter_up = returned[0, 1]
    downward = local_down + passed_down * enter_down[None]
    upward = local_up + passed_up * enter_up[None]
    absorbed = (1.0 - layered_pass) * (downward + upward - 2.0 * layered_emit)
    return (emitted, absorbed.reshape(cell_count, level_count))


def advection(populations, inflow, stream_speed, cross_speed):
    cell_count, level_count = populations.shape
    layered = populations.reshape(cell_count // NY, NY, level_count)
    arrived = shifted(shortened(layered[-1]), "cell", 1)
    boundary = jnp.where(lax.axis_index("cell") == 0, inflow, arrived)
    upstream = jnp.concatenate([boundary[None], layered[:-1]], axis=0)
    before_y = jnp.roll(layered, 1, axis=1)
    after_y = jnp.roll(layered, -1, axis=1)
    along_x = stream_speed.reshape(-1, NY, 1)
    along_y = cross_speed.reshape(-1, NY, 1)
    flux_sum = (
        -along_x * (layered - upstream)
        - jnp.maximum(along_y, 0.0) * (layered - before_y)
        - jnp.minimum(along_y, 0.0) * (after_y - layered)
    )
    return flux_sum.reshape(cell_count, level_count)


def tendency(
    populations,
    rate_blocks,
    pattern,
    bracket,
    cross_section,
    emission,
    absorber,
    stream_speed,
    cross_speed,
    inflow,
):
    rates_part = rate_term(populations, rate_blocks, pattern, bracket)
    emitted, absorbed = radiation(populations, emission, cross_section, absorber)
    carried = advection(populations, inflow, stream_speed, cross_speed)
    return (rates_part - emitted + absorbed + carried, absorbed)


def local(
    populations,
    rate_blocks,
    pattern,
    bracket,
    cross_section,
    emission,
    absorber,
    stream_speed,
    cross_speed,
    inflow,
):
    strips, groups = lax.axis_size("cell"), lax.axis_size("lev")
    cell_count, level_count = populations.shape
    if (
        groups % 2 == 0
        and strips > 1
        and cell_count % NY == 0
        and level_count % (strips * LANES) == 0
        and rate_blocks.shape[3] == LANES
        and 2 * level_count <= strips * LANES * NY
    ):
        advanced, gained = (
            fused(
                strips,
                groups,
                populations,
                rate_blocks,
                pattern,
                bracket,
                cross_section,
                emission,
                absorber,
                stream_speed,
                cross_speed,
                inflow,
            )
        )
        transmit = jnp.exp(-(absorber[:, None] * cross_section[None, :]))
        return (0.5 * (populations + advanced), (1.0 - transmit) * gained)
    first_rate, _ = tendency(
        populations,
        rate_blocks,
        pattern,
        bracket,
        cross_section,
        emission,
        absorber,
        stream_speed,
        cross_speed,
        inflow,
    )
    middle = populations + time_step * first_rate
    second, absorption = tendency(
        middle,
        rate_blocks,
        pattern,
        bracket,
        cross_section,
        emission,
        absorber,
        stream_speed,
        cross_speed,
        inflow,
    )
    updated = 0.5 * (populations + middle + time_step * second)
    return (updated, absorption)


def solution(mesh):
    in_specs = (
        P("cell", "lev"),
        P(None, "lev", None, None, None),
        P("lev", None),
        P("cell"),
        P("lev"),
        P("lev"),
        P("cell"),
        P("cell"),
        P("cell"),
        P(None, "lev"),
    )
    out_specs = (P("cell", "lev"), P("cell", "lev"))
    return jax.shard_map(local, mesh=mesh, in_specs=in_specs, out_specs=out_specs, check_vma=False)
```

profile of v0, /device:TPU:0, one launch (start us, length us, event | category | flops | bytes accessed | tf_op | source)
XLA Modules:
  0.0 35.0 jit_solution(2186723446636526370)
XLA Ops:
  0.6 31.8 %shard_map.113 = (f32[64,2048]{1,0:T(8,128)}, f32[64,2048]{1,0:T(8,128)}) custom-call(s32[6,16]{1,0:T(8,128)} %bitcast.9, f32[64,2048]{1,0:T(8,128)} %p_hbm.1, bf16[2,16,6,128,128]{4,3,2,1,0:T(8,128)(2,1)} %rates_hbm.1, s32[1,64]{1,0:T(1,128)} %bitcast.11, f32[1,64]{1,0:T(1,128)} %bitcast.10, f32[1,64]{1,0:T(1,128)} %bitcast.12, f32[1,64]{1,0:T(1,128)} %bitcast.13, ...), custom_call_target="tpu_custom_call" | custom-call | tf_op jit(solution)/shard_map/pallas_call | solution.py:498
  32.5 2.5 %subtract_multiply_fusion = (f32[64,2048]{1,0:T(8,128)}, f32[64,2048]{1,0:T(8,128)}) fusion(f32[64,2048]{1,0:T(8,128)} %get-tuple-element.5, f32[2048]{0:T(1024)} %param.14, f32[64]{0:T(128)} %param.16, f32[64,2048]{1,0:T(8,128)} %p_hbm.1, f32[64,2048]{1,0:T(8,128)} %get-tuple-element.4), kind=kLoop, calls=%fused_computation | loop fusion | flops 786432 | bytes 2629888 | tf_op jit(solution)/shard_map/mul | solution.py:680
where the time goes:
time: 35.1 us; the launch traced here: 35 us
  Pallas kernels  31.8 us (91%)
  other arithmetic  2.52 us (7%)
  between operations  0.64 us (2%)
    pallas_call x1, Pallas kernels, fused(): pl.pallas_call(functools.partial(fused_kernel, strips, groups), out_shape...  31.8 us
    mul x1, other arithmetic, local(): return (0.5 * (populations + advanced), (1.0 - transmit) * gained)  2.52 us

commit v1 on v0

--- a/solution.py
+++ b/solution.py
@@ -497,7 +497,7 @@
     del held[2]
     return pl.pallas_call(
         functools.partial(fused_kernel, strips, groups),
-        out_shape=[jax.ShapeDtypeStruct((cell_count, level_count), jnp.float32)] * 2,
+        out_shape=[pltpu.VMEM((cell_count, level_count), jnp.float32)] * 2,
         in_specs=[pl.BlockSpec(memory_space=pltpu.HBM)] * len(operands),
         out_specs=[vmem, vmem],
         scratch_shapes=held
@@ -531,9 +531,9 @@
             dma((2, strips)),
         ],
         compiler_params=pltpu.CompilerParams(
-            collective_id=0, has_side_effects=True, vmem_limit_bytes=67043328
+            collective_id=0, has_side_effects=True, vmem_limit_bytes=24 * 1024 * 1024
         ),
-    )(*operands)
+    )(*[pltpu.with_memory_space_constraint(value, pltpu.HBM) for value in operands])
 
 
 def shortened(value):
@@ -558,15 +558,22 @@
     lowered = populations.astype(jnp.bfloat16)
     gathered = lax.all_gather(lowered, "lev", axis=1, tiled=True)
     cell_count = gathered.shape[0]
-    block_size = rate_blocks.shape[3]
-    picked = gathered.reshape(cell_count, -1, block_size)[:, pattern, :]
-    summed = jnp.zeros((cell_count, rate_blocks.shape[1], block_size), jnp.float32)
-    for bracket_id in range(rate_blocks.shape[0]):
-        product = jnp.einsum(
-            "crkj,rkij->cri", picked, rate_blocks[bracket_id], preferred_element_type=jnp.float32
-        )
-        summed = jnp.where((bracket == bracket_id)[:, None, None], product, summed)
-    return summed.reshape(cell_count, -1)
+    brackets, rows, nonzero, block_size = rate_blocks.shape[:4]
+    by_block = jnp.swapaxes(gathered.reshape(cell_count, -1, block_size), 0, 1)
+
+    def one_row(row):
+        summed = jnp.zeros((cell_count, block_size), jnp.float32)
+        for bracket_id in range(brackets):
+            product = jnp.zeros((cell_count, block_size), jnp.float32)
+            for k in range(nonzero):
+                column = lax.dynamic_index_in_dim(by_block, pattern[row, k], 0, keepdims=False)
+                table = lax.dynamic_index_in_dim(rate_blocks[bracket_id], row, 0, keepdims=False)[k]
+                product += jnp.einsum("cj,ij->ci", column, table, preferred_element_type=jnp.float32)
+            summed = jnp.where((bracket == bracket_id)[:, None], product, summed)
+        return summed
+
+    stacked = lax.map(one_row, jnp.arange(rows, dtype=jnp.int32))
+    return jnp.transpose(stacked, (1, 0, 2)).reshape(cell_count, -1)
 
 
 def entering(received):

time: 35.1 us -> 32.8 us (0.934)
  other arithmetic: 2.52 us -> 1.13 us
  Pallas kernels: 31.8 us -> 30.8 us
    mul x1, other arithmetic: 2.52 us -> 1.13 us  [local(): return (0.5 * (populations + advanced), (1.0 - transmit) * gained)]
    pallas_call x1, Pallas kernels: 31.8 us -> 30.8 us  [fused(): pl.pallas_call(functools.partial(fused_kernel, strips, groups), out_shape...]
where the time goes in v1:
time: 32.8 us; the launch traced here: 32.7 us
  Pallas kernels  30.8 us (94%)
  other arithmetic  1.13 us (3%)
  between operations  0.69 us (2%)
    pallas_call x1, Pallas kernels, fused(): pl.pallas_call(functools.partial(fused_kernel, strips, groups), out_shape...  30.8 us
    mul x1, other arithmetic, local(): return (0.5 * (populations + advanced), (1.0 - transmit) * gained)  1.13 us

profile of v1, /device:TPU:0, one launch (start us, length us, event | category | flops | bytes accessed | tf_op | source)
XLA Modules:
  0.0 32.7 jit_solution(5178083233960911438)
XLA Ops:
  0.6 0.0 copy-start.2
  0.6 0.0 copy-start.1
  0.7 0.0 copy-start
  0.7 30.8 %shard_map.113 = (f32[64,2048]{1,0:T(8,128)S(1)}, f32[64,2048]{1,0:T(8,128)S(1)}) custom-call(s32[6,16]{1,0:T(8,128)} %bitcast.9, f32[64,2048]{1,0:T(8,128)} %p_hbm.1, bf16[2,16,6,128,128]{4,3,2,1,0:T(8,128)(2,1)} %rates_hbm.1, s32[1,64]{1,0:T(1,128)} %bitcast.11, f32[1,64]{1,0:T(1,128)} %bitcast.10, f32[1,64]{1,0:T(1,128)} %bitcast.12, f32[1,64]{1,0:T(1,128)} %bitcast.13, ...), custom_call_target="tpu_custom_call" | custom-call | tf_op jit(solution)/shard_map/pallas_call | solution.py:498
  31.5 0.0 copy-done.2
  31.5 0.0 copy-done.1
  31.5 0.0 copy-done
  31.5 1.1 %subtract_multiply_fusion = (f32[64,2048]{1,0:T(8,128)}, f32[64,2048]{1,0:T(8,128)}) fusion(f32[64,2048]{1,0:T(8,128)S(1)} %get-tuple-element.5, f32[2048]{0:T(1024)S(1)} %copy-done.1, f32[64]{0:T(128)S(1)} %copy-done.2, f32[64,2048]{1,0:T(8,128)S(1)} %copy-done, f32[64,2048]{1,0:T(8,128)S(1)} %get-tuple-element.4), kind=kLoop, calls=%fused_computation | loop fusion | flops 786432 | bytes 2629888 | tf_op jit(solution)/shard_map/mul | solution.py:687
Async XLA Ops:
  0.6 30.9 %copy-start.2 = (f32[64]{0:T(128)S(1)}, f32[64]{0:T(128)}, u32[]{:S(2)}) copy-start(f32[64]{0:T(128)} %param.16) | copy-start | bytes 772
  0.6 30.9 %copy-start.1 = (f32[2048]{0:T(1024)S(1)}, f32[2048]{0:T(1024)}, u32[]{:S(2)}) copy-start(f32[2048]{0:T(1024)} %param.14) | copy-start | bytes 24580
  0.7 30.9 %copy-start = (f32[64,2048]{1,0:T(8,128)S(1)}, f32[64,2048]{1,0:T(8,128)}, u32[]{:S(2)}) copy-start(f32[64,2048]{1,0:T(8,128)} %p_hbm.1) | copy-start | bytes 1572868

commit v2 on v1

--- a/solution.py
+++ b/solution.py
@@ -43,14 +43,15 @@
     coef,
     passing,
     middle,
-    rate_sum,
     gathered_first,
     gathered_second,
     halo,
     columns,
-    share_pass,
+    near_pass,
+    far_pass,
     out_one,
-    in_one,
+    in_near,
+    in_far,
     out_two,
     in_two,
     rates_sem,
@@ -58,24 +59,55 @@
     gather_send,
     gather_recv,
     forward_send,
+    partner_send,
+    partner_recv,
     halo_send,
     halo_recv,
     column_send,
     column_recv,
-    one_send,
-    one_recv,
+    near_send,
+    near_recv,
+    far_send,
+    far_recv,
     two_send,
     two_recv,
 ):
     cell = lax.axis_index("cell")
+    lev = lax.axis_index("lev")
     gathered = (gathered_first, gathered_second)
-    lev = lax.axis_index("lev")
     cell_count = p_ref.shape[0]
     layers = cell_count // NY
     blocks = p_ref.shape[1] // LANES
-    per_owner = blocks // strips
+    half = strips // 2
+    piece = blocks // half
     brackets, _, nonzero = rates_hbm.shape[:3]
     partner = lev + 1 - 2 * lax.rem(lev, 2)
+    side = cell // half
+    pos = lax.rem(cell, half)
+    base = side * half
+    other = (1 - side) * half
+    slot = pos + side * (half - 1 - 2 * pos)
+
+    barrier = pltpu.get_barrier_semaphore()
+    greeted = 0
+    for step in range(1, strips):
+        pl.semaphore_signal(
+            barrier,
+            inc=1,
+            device_id={"cell": lax.rem(cell + step, strips), "lev": lev},
+            device_id_type=MESH,
+        )
+        greeted += 1
+    for step in range(1, groups // 2):
+        pl.semaphore_signal(
+            barrier,
+            inc=1,
+            device_id={"cell": cell, "lev": lax.rem(lev + 2 * step, groups)},
+            device_id_type=MESH,
+        )
+        greeted += 1
+    pl.semaphore_signal(barrier, inc=1, device_id={"cell": cell, "lev": partner}, device_id_type=MESH)
+    greeted += 1
 
     operands = [
         pltpu.make_async_copy(source, into, operand_sem.at[index])
@@ -98,27 +130,6 @@
     fetch = pltpu.make_async_copy(rates_hbm, rates, rates_sem)
     fetch.start()
 
-    barrier = pltpu.get_barrier_semaphore()
-    greeted = 0
-    for step in range(1, strips):
-        pl.semaphore_signal(
-            barrier,
-            inc=1,
-            device_id={"cell": lax.rem(cell + step, strips), "lev": lev},
-            device_id_type=MESH,
-        )
-        greeted += 1
-    for step in range(1, groups // 2):
-        pl.semaphore_signal(
-            barrier,
-            inc=1,
-            device_id={"cell": cell, "lev": lax.rem(lev + 2 * step, groups)},
-            device_id_type=MESH,
-        )
-        greeted += 1
-    pl.semaphore_signal(barrier, inc=1, device_id={"cell": cell, "lev": partner}, device_id_type=MESH)
-    greeted += 1
-
     def rows(x):
         return slice(x * NY, (x + 1) * NY)
 
@@ -138,19 +149,29 @@
     def lanes(block):
         return pl.ds(pl.multiple_of(block * LANES, LANES), LANES)
 
-    chunks = gather_recv.shape[2]
-    piece = blocks // chunks
-
-    def own_slot(part, who, chunk):
-        return gathered[part].at[pl.ds(who * blocks + chunk * piece, piece)]
-
-    def gather_copy(part, to, source, send_sem, chunk):
+    def turn_of(index):
+        return lax.rem(pos + 1 + index, half)
+
+    def own_slot(part, who, share):
+        return gathered[part].at[pl.ds(who * blocks + share * piece, piece)]
+
+    def gather_copy(part, to, source, send_sem, share):
         return pltpu.make_async_remote_copy(
-            src_ref=own_slot(part, source, chunk),
-            dst_ref=own_slot(part, source, chunk),
-            send_sem=send_sem.at[chunk],
-            recv_sem=gather_recv.at[part, source, chunk],
+            src_ref=own_slot(part, source, share),
+            dst_ref=own_slot(part, source, share),
+            send_sem=send_sem.at[share],
+            recv_sem=gather_recv.at[part, source, share],
             device_id={"cell": cell, "lev": to},
+            device_id_type=MESH,
+        )
+
+    def partner_copy(part, who):
+        return pltpu.make_async_remote_copy(
+            src_ref=gathered[part].at[pl.ds(who * blocks, blocks)],
+            dst_ref=gathered[part].at[pl.ds(who * blocks, blocks)],
+            send_sem=partner_send.at[part],
+            recv_sem=partner_recv.at[part],
+            device_id={"cell": cell, "lev": partner},
             device_id_type=MESH,
         )
 
@@ -175,14 +196,33 @@
             device_id_type=MESH,
         )
 
-    def strip_copy(part, step, out, into, send_sem, recv_sem):
-        to = lax.rem(cell + step, strips)
+    def near_copy(part, share, who):
         return pltpu.make_async_remote_copy(
-            src_ref=out.at[part, to],
-            dst_ref=into.at[part, cell],
-            send_sem=send_sem.at[part, step],
-            recv_sem=recv_sem.at[part, step],
-            device_id={"cell": to, "lev": lev},
+            src_ref=out_one.at[part, share],
+            dst_ref=in_near.at[part, who],
+            send_sem=near_send.at[part, share],
+            recv_sem=near_recv.at[part, who],
+            device_id={"cell": base + share, "lev": lev},
+            device_id_type=MESH,
+        )
+
+    def far_copy(part, share, who):
+        return pltpu.make_async_remote_copy(
+            src_ref=out_one.at[part, share, side],
+            dst_ref=in_far.at[part, who],
+            send_sem=far_send.at[part, share],
+            recv_sem=far_recv.at[part, who],
+            device_id={"cell": other + share, "lev": lev},
+            device_id_type=MESH,
+        )
+
+    def two_copy(part, to, who):
+        return pltpu.make_async_remote_copy(
+            src_ref=out_two.at[part, to],
+            dst_ref=in_two.at[part, who],
+            send_sem=two_send.at[part, to],
+            recv_sem=two_recv.at[part, who],
+            device_id={"cell": base + to, "lev": lev},
             device_id_type=MESH,
         )
 
@@ -190,28 +230,29 @@
         return value * emission_ref[pl.ds(block, 1), :]
 
     def put(ref, part, index, downs, ups):
-        means = []
-        for place, value in enumerate(downs + ups):
-            mean = jnp.mean(value, axis=0, keepdims=True).astype(jnp.bfloat16).astype(jnp.float32)
-            ref[part, index, place] = (value - mean).astype(jnp.bfloat16)
-            means.append(mean)
-        means.append(jnp.zeros((NY - len(means), LANES), jnp.float32))
-        ref[part, index, 2 * per_owner] = jnp.concatenate(means, axis=0).astype(jnp.bfloat16)
+        for way, values in enumerate((downs, ups)):
+            means = []
+            for place, value in enumerate(values):
+                mean = jnp.mean(value, axis=0, keepdims=True).astype(jnp.bfloat16).astype(jnp.float32)
+                ref[part, index, way, place] = (value - mean).astype(jnp.bfloat16)
+                means.append(mean)
+            means.append(jnp.zeros((NY - len(means), LANES), jnp.float32))
+            ref[part, index, way, piece] = jnp.concatenate(means, axis=0).astype(jnp.bfloat16)
+
+    def got(message, b):
+        means = message[piece].astype(jnp.float32)
+        return message[b].astype(jnp.float32) + means[b : b + 1]
 
     def get(ref, part, index, b):
-        means = ref[part, index, 2 * per_owner].astype(jnp.float32)
-        return tuple(
-            ref[part, index, place].astype(jnp.float32) + means[place : place + 1]
-            for place in (b, per_owner + b)
-        )
+        return tuple(got(ref.at[part, index, way], b) for way in range(2))
 
     def lower(part, block, value):
         gathered[part][lev * blocks + block] = value.astype(jnp.bfloat16)
 
-    def summarize(part, owner, values):
+    def summarize(part, share, values):
         downs, ups = [], []
-        for b in range(per_owner):
-            block = owner * per_owner + b
+        for b in range(piece):
+            block = share * piece + b
             through = [passing[block, rows(x), :] for x in range(layers)]
             emit = [emitted_of(values[b][x], block) for x in range(layers)]
             down, up = emit[0], emit[-1]
@@ -220,16 +261,26 @@
                 up = through[layers - 1 - x] * up + emit[layers - 1 - x]
             downs.append(down)
             ups.append(up)
-        put(out_one, part, owner, downs, ups)
+        put(out_one, part, share, downs, ups)
+
+    def send_summary(part, share):
+        far_copy(part, share, slot).start()
+
+        @pl.when(share != pos)
+        def _():
+            near_copy(part, share, pos).start()
+
+        @pl.when(share == pos)
+        def _():
+            in_near[part, pos] = out_one[part, pos]
 
     def load_start(block):
         return [p_ref[rows(x), lanes(block)] for x in range(layers)]
 
-    def start_gather(part, chunk):
+    def start_gather(part, share):
         for step in range(1, groups // 2):
             to = lax.rem(lev + 2 * step, groups)
-            gather_copy(part, to, lev, gather_send.at[part, step], chunk).start()
-        gather_copy(part, partner, lev, gather_send.at[part, 0], chunk).start()
+            gather_copy(part, to, lev, gather_send.at[part, step], share).start()
 
     def start_halo(part):
         @pl.when(cell < strips - 1)
@@ -241,12 +292,13 @@
         return 0
 
     operands[0].wait()
+    lax.fori_loop(0, blocks, lower_start, 0, unroll=4)
     operands[1].wait()
     columns[cell] = absorber_ref[...]
     pl.semaphore_wait(barrier, greeted)
-    for chunk in range(chunks):
-        lax.fori_loop(chunk * piece, (chunk + 1) * piece, lower_start, 0, unroll=2)
-        start_gather(0, chunk)
+    for index in range(half):
+        start_gather(0, turn_of(index))
+    partner_copy(0, lev).start()
     for step in range(1, strips):
         column_copy(step).start()
 
@@ -254,109 +306,125 @@
         copy.wait()
     coef[0] = spread(absorber_ref[...])
 
-    def pass_block(block, _):
-        passing[block] = jnp.exp(-(coef[0] * cross_ref[pl.ds(block, 1), :]))
+    def summarize_start(index, _):
+        share = turn_of(index)
+        values = []
+        for b in range(piece):
+            block = share * piece + b
+            passing[block] = jnp.exp(-(coef[0] * cross_ref[pl.ds(block, 1), :]))
+            values.append(load_start(block))
+        summarize(0, share, values)
+        send_summary(0, share)
         return 0
 
-    def summarize_start(owner, _):
-        values = []
-        for b in range(per_owner):
-            pass_block(owner * per_owner + b, 0)
-            values.append(load_start(owner * per_owner + b))
-        summarize(0, owner, values)
-        return 0
-
-    lax.fori_loop(0, strips, summarize_start, 0)
-
-    def start_one(part):
-        for step in range(1, strips):
-            strip_copy(part, step, out_one, in_one, one_send, one_recv).start()
-        in_one[part, cell] = out_one[part, cell]
-
-    start_one(0)
+    lax.fori_loop(0, half, summarize_start, 0)
     start_halo(0)
     coef[1] = spread(stream_ref[...])
     coef[2] = spread(turn_ref[...])
     coef[3] = spread(bracket_ref[...].astype(jnp.float32))
+
+    @pl.when(cell == 0)
+    def _():
+        for part in range(2):
+            for block in range(blocks):
+                halo[part, block] = inflow_ref[:, block * LANES : (block + 1) * LANES].astype(
+                    jnp.bfloat16
+                )
+
+    fetch.wait()
+
+    def turn_tables(row, _):
+        for bracket in range(brackets):
+            for k in range(nonzero):
+                rates[bracket, row, k] = rates[bracket, row, k].T
+        return 0
+
+    lax.fori_loop(0, blocks, turn_tables, 0, unroll=2)
     for step in range(1, strips):
         column_copy(step).wait()
 
-    def share_block(strip, _):
-        column = summed_layers(columns[strip])
-        for b in range(per_owner):
-            cross = cross_ref[pl.ds(cell * per_owner + b, 1), :]
-            share_pass[strip, b] = jnp.exp(-(column * cross))
+    def share_block(index, _):
+        near = summed_layers(columns[base + index])
+        far = summed_layers(columns[other + index + (1 - side) * (half - 1 - 2 * index)])
+        for b in range(piece):
+            cross = cross_ref[pl.ds(pos * piece + b, 1), :]
+            near_pass[index, b] = jnp.exp(-(near * cross))
+            far_pass[index, b] = jnp.exp(-(far * cross))
         return 0
 
-    lax.fori_loop(0, strips, share_block, 0)
+    lax.fori_loop(0, half, share_block, 0)
 
     def enter(part):
-        for step in range(1, strips):
-            strip_copy(part, step, out_one, in_one, one_send, one_recv).wait()
-        below = [[] for _ in range(strips)]
-        above = [[] for _ in range(strips)]
-        for b in range(per_owner):
-            parts = [get(in_one, part, strip, b) for strip in range(strips)]
-            running = jnp.zeros((NY, LANES), jnp.float32)
-            for strip in range(strips):
-                below[strip].append(running)
-                running = share_pass[strip, b] * running + parts[strip][0]
-            running = jnp.zeros((NY, LANES), jnp.float32)
-            for strip in reversed(range(strips)):
-                above[strip].append(running)
-                running = share_pass[strip, b] * running + parts[strip][1]
-        for strip in range(strips):
-            put(out_two, part, strip, below[strip], above[strip])
-        for step in range(1, strips):
-            strip_copy(part, step, out_two, in_two, two_send, two_recv).start()
-        in_two[part, cell] = out_two[part, cell]
-
-    def forward(part, chunk):
+        for index in range(half):
+            far_copy(part, index, index).wait_recv()
+        for step in range(1, half):
+            near_copy(part, pos, lax.rem(pos + step, half)).wait_recv()
+        below = [[] for _ in range(half)]
+        above = [[] for _ in range(half)]
+        for b in range(piece):
+            beyond = jnp.zeros((NY, LANES), jnp.float32)
+            for index in range(half):
+                beyond = far_pass[index, b] * beyond + got(in_far.at[part, index], b)
+            parts = [get(in_near, part, index, b) for index in range(half)]
+            running = jnp.where(side == 1, beyond, 0.0)
+            for index in range(half):
+                below[index].append(running)
+                running = near_pass[index, b] * running + parts[index][0]
+            running = jnp.where(side == 0, beyond, 0.0)
+            for index in reversed(range(half)):
+                above[index].append(running)
+                running = near_pass[index, b] * running + parts[index][1]
+        for index in range(half):
+            put(out_two, part, index, below[index], above[index])
+        for step in range(1, half):
+            two_copy(part, lax.rem(pos + step, half), pos).start()
+        in_two[part, pos] = out_two[part, pos]
+
+    def forward(part, share):
         for step in range(1, groups // 2):
             source = lax.rem(lev + 2 * step, groups)
-            gather_copy(part, lev, source, gather_send.at[part, step], chunk).wait_recv()
-            gather_copy(part, partner, source, forward_send.at[part, step], chunk).start()
-
-    def rates_of(part):
-        for chunk in range(chunks):
-            gather_copy(part, partner, partner, gather_send.at[part, 0], chunk).wait_recv()
+            gather_copy(part, lev, source, gather_send.at[part, step], share).wait_recv()
+            gather_copy(part, partner, source, forward_send.at[part, step], share).start()
+
+    def all_gathered(part):
+        partner_copy(part, partner).wait_recv()
+        for index in range(half):
             for step in range(1, groups // 2):
                 source = lax.rem(partner + 2 * step, groups)
-                gather_copy(part, lev, source, gather_send.at[part, step], chunk).wait_recv()
-
-        def one_row(row, _):
-            picked = jnp.concatenate(
-                [gathered[part][pattern_ref[k, row]] for k in range(nonzero)], axis=1
+                gather_copy(part, lev, source, gather_send.at[part, step], turn_of(index)).wait_recv()
+
+    def rate_of(part, row):
+        picked = jnp.concatenate(
+            [gathered[part][pattern_ref[k, row]] for k in range(nonzero)], axis=1
+        )
+        table = jnp.concatenate(
+            [
+                jnp.concatenate([rates[bracket, row, k] for k in range(nonzero)], axis=0)
+                for bracket in range(brackets)
+            ],
+            axis=1,
+        )
+        product = jnp.dot(picked, table, preferred_element_type=jnp.float32)
+        kind = coef[3]
+        summed = product[:, :LANES]
+        for bracket in range(1, brackets):
+            summed = jnp.where(
+                kind == float(bracket),
+                product[:, bracket * LANES : (bracket + 1) * LANES],
+                summed,
             )
-            table = jnp.concatenate(
-                [
-                    jnp.concatenate([rates[bracket, row, k] for k in range(nonzero)], axis=1)
-                    for bracket in range(brackets)
-                ],
-                axis=0,
-            )
-            product = lax.dot_general(
-                picked, table, (((1,), (1,)), ((), ())), preferred_element_type=jnp.float32
-            )
-            kind = coef[3]
-            summed = product[:, :LANES]
-            for bracket in range(1, brackets):
-                summed = jnp.where(
-                    kind == float(bracket),
-                    product[:, bracket * LANES : (bracket + 1) * LANES],
-                    summed,
-                )
-            rate_sum[row] = summed
-            return 0
-
-        lax.fori_loop(0, blocks, one_row, 0, unroll=4)
+        return summed
 
     def finish_transfers(part):
-        for chunk in range(chunks):
+        partner_copy(part, lev).wait_send()
+        for index in range(half):
             for step in range(1, groups // 2):
-                gather_copy(part, partner, lev, gather_send.at[part, step], chunk).wait_send()
-                gather_copy(part, partner, lev, forward_send.at[part, step], chunk).wait_send()
-            gather_copy(part, partner, lev, gather_send.at[part, 0], chunk).wait_send()
+                gather_copy(part, partner, lev, gather_send.at[part, step], index).wait_send()
+                gather_copy(part, partner, lev, forward_send.at[part, step], index).wait_send()
+            far_copy(part, index, slot).wait_send()
+        for step in range(1, half):
+            near_copy(part, lax.rem(pos + step, half), pos).wait_send()
+            two_copy(part, lax.rem(pos + step, half), pos).wait_send()
 
         @pl.when(cell < strips - 1)
         def _():
@@ -367,21 +435,12 @@
         def _():
             halo_copy(part).wait_recv()
 
-        @pl.when(cell == 0)
-        def _():
-            for block in range(blocks):
-                halo[part, block] = inflow_ref[:, block * LANES : (block + 1) * LANES].astype(
-                    jnp.bfloat16
-                )
-
-        for step in range(1, strips):
-            strip_copy(part, step, out_two, in_two, two_send, two_recv).wait()
-
-    def tendency(part, owner, b, value):
-        block = owner * per_owner + b
+    def tendency(part, share, b, value):
+        block = share * piece + b
         through = [passing[block, rows(x), :] for x in range(layers)]
         emit = [emitted_of(value[x], block) for x in range(layers)]
-        down, up = get(in_two, part, owner, b)
+        rate_sum = rate_of(part, block)
+        down, up = get(in_two, part, share, b)
         downs, ups = [None] * layers, [None] * layers
         for x in range(layers):
             down = through[x] * down + emit[x]
@@ -405,57 +464,64 @@
                 - jnp.minimum(cross, 0.0) * (after_y - value[x])
             )
             gains.append(gained)
-            total.append(rate_sum[block, rows(x), :] - emit[x] + taken + carried)
+            total.append(rate_sum[rows(x)] - emit[x] + taken + carried)
         return gains, total
 
     def exchange(part):
-        for chunk in range(chunks - 1):
-            forward(part, chunk)
+        early = half // 2
+        for index in range(early):
+            forward(part, turn_of(index))
         enter(part)
-        forward(part, chunks - 1)
+        for index in range(early, half):
+            forward(part, turn_of(index))
+        all_gathered(part)
+        before_close(part)
+
+    def arrived_two(part, share):
+        @pl.when(share != pos)
+        def _():
+            two_copy(part, pos, share).wait_recv()
 
     exchange(0)
-    fetch.wait()
-    rates_of(0)
-    before_close(0)
-
-    def close_first(owner, _):
+
+    def close_first(index, _):
+        share = turn_of(index)
+        arrived_two(0, share)
         values = []
-        for b in range(per_owner):
-            block = owner * per_owner + b
+        for b in range(piece):
+            block = share * piece + b
             value = load_start(block)
-            _, total = tendency(0, owner, b, value)
+            _, total = tendency(0, share, b, value)
             renewed = [value[x] + time_step * total[x] for x in range(layers)]
             for x in range(layers):
                 middle[block, rows(x), :] = renewed[x]
             lower(1, block, jnp.concatenate(renewed, axis=0))
             values.append(renewed)
-        summarize(1, owner, values)
+        start_gather(1, share)
+        summarize(1, share, values)
+        send_summary(1, share)
         return 0
 
-    owners = strips // chunks
-    for chunk in range(chunks):
-        lax.fori_loop(chunk * owners, (chunk + 1) * owners, close_first, 0)
-        start_gather(1, chunk)
-    start_one(1)
+    lax.fori_loop(0, half, close_first, 0)
+    partner_copy(1, lev).start()
     start_halo(1)
     finish_transfers(0)
     exchange(1)
-    rates_of(1)
-    before_close(1)
-
-    def close_second(owner, _):
-        for b in range(per_owner):
-            block = owner * per_owner + b
+    finish_transfers(1)
+
+    def close_second(index, _):
+        share = lax.rem(pos + index, half)
+        arrived_two(1, share)
+        for b in range(piece):
+            block = share * piece + b
             value = [middle[block, rows(x), :] for x in range(layers)]
-            gains, total = tendency(1, owner, b, value)
+            gains, total = tendency(1, share, b, value)
             for x in range(layers):
                 gained_ref[rows(x), lanes(block)] = gains[x]
                 advanced_ref[rows(x), lanes(block)] = value[x] + time_step * total[x]
         return 0
 
-    lax.fori_loop(0, strips, close_second, 0)
-    finish_transfers(1)
+    lax.fori_loop(0, half, close_second, 0)
 
 
 def fused(
@@ -474,10 +540,10 @@
 ):
     cell_count, level_count = populations.shape
     blocks = level_count // LANES
-    per_owner = blocks // strips
-    chunks = 4 if strips % 4 == 0 else 1
+    half = strips // 2
+    piece = blocks // half
     layers_shape = (blocks, cell_count, LANES)
-    share = (2, strips, 2 * per_owner + 1, NY, LANES)
+    message = (2, piece + 1, NY, LANES)
     vmem = pl.BlockSpec(memory_space=pltpu.VMEM)
     dma = pltpu.SemaphoreType.DMA
     operands = [
@@ -506,29 +572,34 @@
             pltpu.VMEM((4, cell_count, LANES), jnp.float32),
             pltpu.VMEM(layers_shape, jnp.float32),
             pltpu.VMEM(layers_shape, jnp.float32),
-            pltpu.VMEM(layers_shape, jnp.float32),
             pltpu.VMEM((groups * blocks, cell_count, LANES), jnp.bfloat16),
             pltpu.VMEM((groups * blocks, cell_count, LANES), jnp.bfloat16),
             pltpu.VMEM((2, blocks, NY, LANES), jnp.bfloat16),
             pltpu.VMEM((strips, 1, cell_count), jnp.float32),
-            pltpu.VMEM((strips, per_owner, NY, LANES), jnp.float32),
-            pltpu.VMEM(share, jnp.bfloat16),
-            pltpu.VMEM(share, jnp.bfloat16),
-            pltpu.VMEM(share, jnp.bfloat16),
-            pltpu.VMEM(share, jnp.bfloat16),
+            pltpu.VMEM((half, piece, NY, LANES), jnp.float32),
+            pltpu.VMEM((half, piece, NY, LANES), jnp.float32),
+            pltpu.VMEM((2, half) + message, jnp.bfloat16),
+            pltpu.VMEM((2, half) + message, jnp.bfloat16),
+            pltpu.VMEM((2, half) + message[1:], jnp.bfloat16),
+            pltpu.VMEM((2, half) + message, jnp.bfloat16),
+            pltpu.VMEM((2, half) + message, jnp.bfloat16),
             dma(()),
             dma((len(held),)),
-            dma((2, groups, chunks)),
-            dma((2, groups, chunks)),
-            dma((2, groups, chunks)),
+            dma((2, groups, half)),
+            dma((2, groups, half)),
+            dma((2, groups, half)),
+            dma((2,)),
+            dma((2,)),
             dma((2,)),
             dma((2,)),
             dma((strips,)),
             dma((strips,)),
-            dma((2, strips)),
-            dma((2, strips)),
-            dma((2, strips)),
-            dma((2, strips)),
+            dma((2, half)),
+            dma((2, half)),
+            dma((2, half)),
+            dma((2, half)),
+            dma((2, half)),
+            dma((2, half)),
         ],
         compiler_params=pltpu.CompilerParams(
             collective_id=0, has_side_effects=True, vmem_limit_bytes=24 * 1024 * 1024
@@ -661,11 +732,11 @@
     cell_count, level_count = populations.shape
     if (
         groups % 2 == 0
-        and strips > 1
+        and strips % 2 == 0
         and cell_count % NY == 0
-        and level_count % (strips * LANES) == 0
+        and level_count % (strips // 2 * LANES) == 0
         and rate_blocks.shape[3] == LANES
-        and 2 * level_count <= strips * LANES * NY
+        and 2 * level_count < strips * LANES * NY
     ):
         advanced, gained = (
             fused(

time: 32.8 us -> 29.3 us (0.89)
  Pallas kernels: 30.8 us -> 27.3 us
    pallas_call x1, Pallas kernels: 30.8 us -> 27.3 us  [fused(): pl.pallas_call(functools.partial(fused_kernel, strips, groups), out_shape...]
where the time goes in v2:
time: 29.3 us; the launch traced here: 29.2 us
  Pallas kernels  27.3 us (93%)
  other arithmetic  1.13 us (4%)
  between operations  0.69 us (2%)
    pallas_call x1, Pallas kernels, fused(): pl.pallas_call(functools.partial(fused_kernel, strips, groups), out_shape...  27.3 us
    mul x1, other arithmetic, local(): return (0.5 * (populations + advanced), (1.0 - transmit) * gained)  1.13 us

profile of v2, /device:TPU:0, one launch (start us, length us, event | category | flops | bytes accessed | tf_op | source)
XLA Modules:
  0.0 29.2 jit_solution(3208190327975533952)
XLA Ops:
  0.6 0.0 copy-start.2
  0.6 0.0 copy-start.1
  0.7 0.0 copy-start
  0.7 27.3 %shard_map.113 = (f32[64,2048]{1,0:T(8,128)S(1)}, f32[64,2048]{1,0:T(8,128)S(1)}) custom-call(s32[6,16]{1,0:T(8,128)} %bitcast.9, f32[64,2048]{1,0:T(8,128)} %p_hbm.1, bf16[2,16,6,128,128]{4,3,2,1,0:T(8,128)(2,1)} %rates_hbm.1, s32[1,64]{1,0:T(1,128)} %bitcast.11, f32[1,64]{1,0:T(1,128)} %bitcast.10, f32[1,64]{1,0:T(1,128)} %bitcast.12, f32[1,64]{1,0:T(1,128)} %bitcast.13, ...), custom_call_target="tpu_custom_call" | custom-call | tf_op jit(solution)/shard_map/pallas_call | solution.py:564
  28.0 0.0 copy-done.2
  28.0 0.0 copy-done.1
  28.0 0.0 copy-done
  28.0 1.1 %subtract_multiply_fusion = (f32[64,2048]{1,0:T(8,128)}, f32[64,2048]{1,0:T(8,128)}) fusion(f32[64,2048]{1,0:T(8,128)S(1)} %get-tuple-element.5, f32[2048]{0:T(1024)S(1)} %copy-done.1, f32[64]{0:T(128)S(1)} %copy-done.2, f32[64,2048]{1,0:T(8,128)S(1)} %copy-done, f32[64,2048]{1,0:T(8,128)S(1)} %get-tuple-element.4), kind=kLoop, calls=%fused_computation | loop fusion | flops 786432 | bytes 2629888 | tf_op jit(solution)/shard_map/mul | solution.py:758
Async XLA Ops:
  0.6 27.4 %copy-start.2 = (f32[64]{0:T(128)S(1)}, f32[64]{0:T(128)}, u32[]{:S(2)}) copy-start(f32[64]{0:T(128)} %param.16) | copy-start | bytes 772
  0.6 27.4 %copy-start.1 = (f32[2048]{0:T(1024)S(1)}, f32[2048]{0:T(1024)}, u32[]{:S(2)}) copy-start(f32[2048]{0:T(1024)} %param.14) | copy-start | bytes 24580
  0.7 27.4 %copy-start = (f32[64,2048]{1,0:T(8,128)S(1)}, f32[64,2048]{1,0:T(8,128)}, u32[]{:S(2)}) copy-start(f32[64,2048]{1,0:T(8,128)} %p_hbm.1) | copy-start | bytes 1572868

commit v3 on v2

--- a/solution.py
+++ b/solution.py
@@ -208,7 +208,7 @@
 
     def far_copy(part, share, who):
         return pltpu.make_async_remote_copy(
-            src_ref=out_one.at[part, share, side],
+            src_ref=out_one.at[part, share, pl.ds(piece * side, piece)],
             dst_ref=in_far.at[part, who],
             send_sem=far_send.at[part, share],
             recv_sem=far_recv.at[part, who],
@@ -230,21 +230,35 @@
         return value * emission_ref[pl.ds(block, 1), :]
 
     def put(ref, part, index, downs, ups):
-        for way, values in enumerate((downs, ups)):
-            means = []
-            for place, value in enumerate(values):
-                mean = jnp.mean(value, axis=0, keepdims=True).astype(jnp.bfloat16).astype(jnp.float32)
-                ref[part, index, way, place] = (value - mean).astype(jnp.bfloat16)
-                means.append(mean)
+        means = []
+        for place, value in enumerate(downs + ups):
+            mean = jnp.mean(value, axis=0, keepdims=True).astype(jnp.bfloat16).astype(jnp.float32)
+            ref[part, index, place + place // piece] = (value - mean).astype(jnp.bfloat16)
+            means.append(mean)
+        if len(means) < NY:
             means.append(jnp.zeros((NY - len(means), LANES), jnp.float32))
-            ref[part, index, way, piece] = jnp.concatenate(means, axis=0).astype(jnp.bfloat16)
-
-    def got(message, b):
-        means = message[piece].astype(jnp.float32)
-        return message[b].astype(jnp.float32) + means[b : b + 1]
+        ref[part, index, piece] = jnp.concatenate(means, axis=0).astype(jnp.bfloat16)
 
     def get(ref, part, index, b):
-        return tuple(got(ref.at[part, index, way], b) for way in range(2))
+        means = ref[part, index, piece].astype(jnp.float32)
+        return tuple(
+            ref[part, index, place + place // piece].astype(jnp.float32) + means[place : place + 1]
+            for place in (b, piece + b)
+        )
+
+    def is_first():
+        return lax.broadcasted_iota(jnp.int32, (NY, LANES), 0) == 0
+
+    def put_sums(part, share, downs, ups):
+        for place, value in enumerate(downs + ups):
+            first = value[:1].astype(jnp.bfloat16).astype(jnp.float32)
+            out_one[part, share, place] = jnp.where(is_first(), value, value - first).astype(
+                jnp.bfloat16
+            )
+
+    def restored(tile):
+        value = tile.astype(jnp.float32)
+        return jnp.where(is_first(), value, value + value[:1])
 
     def lower(part, block, value):
         gathered[part][lev * blocks + block] = value.astype(jnp.bfloat16)
@@ -261,7 +275,7 @@
                 up = through[layers - 1 - x] * up + emit[layers - 1 - x]
             downs.append(down)
             ups.append(up)
-        put(out_one, part, share, downs, ups)
+        put_sums(part, share, downs, ups)
 
     def send_summary(part, share):
         far_copy(part, share, slot).start()
@@ -290,21 +304,6 @@
     def lower_start(block, _):
         lower(0, block, p_ref[:, lanes(block)])
         return 0
-
-    operands[0].wait()
-    lax.fori_loop(0, blocks, lower_start, 0, unroll=4)
-    operands[1].wait()
-    columns[cell] = absorber_ref[...]
-    pl.semaphore_wait(barrier, greeted)
-    for index in range(half):
-        start_gather(0, turn_of(index))
-    partner_copy(0, lev).start()
-    for step in range(1, strips):
-        column_copy(step).start()
-
-    for copy in operands[2:]:
-        copy.wait()
-    coef[0] = spread(absorber_ref[...])
 
     def summarize_start(index, _):
         share = turn_of(index)
@@ -314,10 +313,26 @@
             passing[block] = jnp.exp(-(coef[0] * cross_ref[pl.ds(block, 1), :]))
             values.append(load_start(block))
         summarize(0, share, values)
-        send_summary(0, share)
         return 0
 
+    for copy in operands[:4]:
+        copy.wait()
+    lax.fori_loop(0, blocks, lower_start, 0, unroll=4)
+    columns[cell] = absorber_ref[...]
+    coef[0] = spread(absorber_ref[...])
     lax.fori_loop(0, half, summarize_start, 0)
+    pl.semaphore_wait(barrier, greeted)
+    for step in range(1, strips):
+        column_copy(step).start()
+    start_gather(0, turn_of(0))
+    for index in range(half):
+        send_summary(0, turn_of(index))
+    start_gather(0, turn_of(1))
+    for index in range(2, half):
+        start_gather(0, turn_of(index))
+    partner_copy(0, lev).start()
+    for copy in operands[4:]:
+        copy.wait()
     start_halo(0)
     coef[1] = spread(stream_ref[...])
     coef[2] = spread(turn_ref[...])
@@ -364,8 +379,11 @@
         for b in range(piece):
             beyond = jnp.zeros((NY, LANES), jnp.float32)
             for index in range(half):
-                beyond = far_pass[index, b] * beyond + got(in_far.at[part, index], b)
-            parts = [get(in_near, part, index, b) for index in range(half)]
+                beyond = far_pass[index, b] * beyond + restored(in_far[part, index, b])
+            parts = [
+                (restored(in_near[part, index, b]), restored(in_near[part, index, piece + b]))
+                for index in range(half)
+            ]
             running = jnp.where(side == 1, beyond, 0.0)
             for index in range(half):
                 below[index].append(running)
@@ -393,7 +411,7 @@
                 source = lax.rem(partner + 2 * step, groups)
                 gather_copy(part, lev, source, gather_send.at[part, step], turn_of(index)).wait_recv()
 
-    def rate_of(part, row):
+    def rate_row(part, row):
         picked = jnp.concatenate(
             [gathered[part][pattern_ref[k, row]] for k in range(nonzero)], axis=1
         )
@@ -435,11 +453,13 @@
         def _():
             halo_copy(part).wait_recv()
 
-    def tendency(part, share, b, value):
+    def rates_of(part, share):
+        return [rate_row(part, share * piece + b) for b in range(piece)]
+
+    def tendency(part, share, b, value, rate_sum):
         block = share * piece + b
         through = [passing[block, rows(x), :] for x in range(layers)]
         emit = [emitted_of(value[x], block) for x in range(layers)]
-        rate_sum = rate_of(part, block)
         down, up = get(in_two, part, share, b)
         downs, ups = [None] * layers, [None] * layers
         for x in range(layers):
@@ -484,14 +504,13 @@
 
     exchange(0)
 
-    def close_first(index, _):
-        share = turn_of(index)
+    def close_first(share, sums):
         arrived_two(0, share)
         values = []
         for b in range(piece):
             block = share * piece + b
             value = load_start(block)
-            _, total = tendency(0, share, b, value)
+            _, total = tendency(0, share, b, value, sums[b])
             renewed = [value[x] + time_step * total[x] for x in range(layers)]
             for x in range(layers):
                 middle[block, rows(x), :] = renewed[x]
@@ -500,28 +519,36 @@
         start_gather(1, share)
         summarize(1, share, values)
         send_summary(1, share)
-        return 0
-
-    lax.fori_loop(0, half, close_first, 0)
+
+    ready = [rates_of(0, turn_of(index)) for index in range(min(2, half))]
+    for index in range(half):
+        if index + 2 < half:
+            ready.append(rates_of(0, turn_of(index + 2)))
+        close_first(turn_of(index), ready[index])
     partner_copy(1, lev).start()
     start_halo(1)
     finish_transfers(0)
     exchange(1)
     finish_transfers(1)
 
-    def close_second(index, _):
-        share = lax.rem(pos + index, half)
+    def close_second(share, sums):
         arrived_two(1, share)
         for b in range(piece):
             block = share * piece + b
             value = [middle[block, rows(x), :] for x in range(layers)]
-            gains, total = tendency(1, share, b, value)
+            gains, total = tendency(1, share, b, value, sums[b])
             for x in range(layers):
                 gained_ref[rows(x), lanes(block)] = gains[x]
                 advanced_ref[rows(x), lanes(block)] = value[x] + time_step * total[x]
-        return 0
-
-    lax.fori_loop(0, half, close_second, 0)
+
+    def own_first(index):
+        return lax.rem(pos + index, half)
+
+    ready = [rates_of(1, own_first(index)) for index in range(min(2, half))]
+    for index in range(half):
+        if index + 2 < half:
+            ready.append(rates_of(1, own_first(index + 2)))
+        close_second(own_first(index), ready[index])
 
 
 def fused(
@@ -543,7 +570,7 @@
     half = strips // 2
     piece = blocks // half
     layers_shape = (blocks, cell_count, LANES)
-    message = (2, piece + 1, NY, LANES)
+    message = (2 * piece + 1, NY, LANES)
     vmem = pl.BlockSpec(memory_space=pltpu.VMEM)
     dma = pltpu.SemaphoreType.DMA
     operands = [
@@ -578,9 +605,9 @@
             pltpu.VMEM((strips, 1, cell_count), jnp.float32),
             pltpu.VMEM((half, piece, NY, LANES), jnp.float32),
             pltpu.VMEM((half, piece, NY, LANES), jnp.float32),
-            pltpu.VMEM((2, half) + message, jnp.bfloat16),
-            pltpu.VMEM((2, half) + message, jnp.bfloat16),
-            pltpu.VMEM((2, half) + message[1:], jnp.bfloat16),
+            pltpu.VMEM((2, half, 2 * piece, NY, LANES), jnp.bfloat16),
+            pltpu.VMEM((2, half, 2 * piece, NY, LANES), jnp.bfloat16),
+            pltpu.VMEM((2, half, piece, NY, LANES), jnp.bfloat16),
             pltpu.VMEM((2, half) + message, jnp.bfloat16),
             pltpu.VMEM((2, half) + message, jnp.bfloat16),
             dma(()),
@@ -736,7 +763,7 @@
         and cell_count % NY == 0
         and level_count % (strips // 2 * LANES) == 0
         and rate_blocks.shape[3] == LANES
-        and 2 * level_count < strips * LANES * NY
+        and 4 * level_count <= strips * LANES * NY
     ):
         advanced, gained = (
             fused(

time: 29.3 us -> 28.3 us (0.966)
  Pallas kernels: 27.3 us -> 26.4 us
    pallas_call x1, Pallas kernels: 27.3 us -> 26.4 us  [fused(): pl.pallas_call(functools.partial(fused_kernel, strips, groups), out_shape...]
where the time goes in v3:
time: 28.3 us; the launch traced here: 28.2 us
  Pallas kernels  26.4 us (93%)
  other arithmetic  1.13 us (4%)
  between operations  0.69 us (2%)
    pallas_call x1, Pallas kernels, fused(): pl.pallas_call(functools.partial(fused_kernel, strips, groups), out_shape...  26.4 us
    mul x1, other arithmetic, local(): return (0.5 * (populations + advanced), (1.0 - transmit) * gained)  1.13 us

profile of v3, /device:TPU:0, one launch (start us, length us, event | category | flops | bytes accessed | tf_op | source)
XLA Modules:
  0.0 28.2 jit_solution(1305617298361188730)
XLA Ops:
  0.6 0.0 copy-start.2
  0.6 0.0 copy-start.1
  0.7 0.0 copy-start
  0.7 26.4 %shard_map.113 = (f32[64,2048]{1,0:T(8,128)S(1)}, f32[64,2048]{1,0:T(8,128)S(1)}) custom-call(s32[6,16]{1,0:T(8,128)} %bitcast.9, f32[64,2048]{1,0:T(8,128)} %p_hbm.1, bf16[2,16,6,128,128]{4,3,2,1,0:T(8,128)(2,1)} %rates_hbm.1, s32[1,64]{1,0:T(1,128)} %bitcast.11, f32[1,64]{1,0:T(1,128)} %bitcast.10, f32[1,64]{1,0:T(1,128)} %bitcast.12, f32[1,64]{1,0:T(1,128)} %bitcast.13, ...), custom_call_target="tpu_custom_call" | custom-call | tf_op jit(solution)/shard_map/pallas_call | solution.py:591
  27.0 0.0 copy-done.2
  27.0 0.0 copy-done.1
  27.1 0.0 copy-done
  27.1 1.1 %subtract_multiply_fusion = (f32[64,2048]{1,0:T(8,128)}, f32[64,2048]{1,0:T(8,128)}) fusion(f32[64,2048]{1,0:T(8,128)S(1)} %get-tuple-element.5, f32[2048]{0:T(1024)S(1)} %copy-done.1, f32[64]{0:T(128)S(1)} %copy-done.2, f32[64,2048]{1,0:T(8,128)S(1)} %copy-done, f32[64,2048]{1,0:T(8,128)S(1)} %get-tuple-element.4), kind=kLoop, calls=%fused_computation | loop fusion | flops 786432 | bytes 2629888 | tf_op jit(solution)/shard_map/mul | solution.py:785
Async XLA Ops:
  0.6 26.4 %copy-start.2 = (f32[64]{0:T(128)S(1)}, f32[64]{0:T(128)}, u32[]{:S(2)}) copy-start(f32[64]{0:T(128)} %param.16) | copy-start | bytes 772
  0.6 26.4 %copy-start.1 = (f32[2048]{0:T(1024)S(1)}, f32[2048]{0:T(1024)}, u32[]{:S(2)}) copy-start(f32[2048]{0:T(1024)} %param.14) | copy-start | bytes 24580
  0.7 26.4 %copy-start = (f32[64,2048]{1,0:T(8,128)S(1)}, f32[64,2048]{1,0:T(8,128)}, u32[]{:S(2)}) copy-start(f32[64,2048]{1,0:T(8,128)} %p_hbm.1) | copy-start | bytes 1572868

commit v4 on v3

--- a/solution.py
+++ b/solution.py
@@ -43,6 +43,10 @@
     coef,
     passing,
     middle,
+    known,
+    inside,
+    from_below,
+    from_above,
     gathered_first,
     gathered_second,
     halo,
@@ -291,6 +295,9 @@
     def load_start(block):
         return [p_ref[rows(x), lanes(block)] for x in range(layers)]
 
+    def load_middle(block):
+        return [middle[block, rows(x), :] for x in range(layers)]
+
     def start_gather(part, share):
         for step in range(1, groups // 2):
             to = lax.rem(lev + 2 * step, groups)
@@ -456,62 +463,85 @@
     def rates_of(part, share):
         return [rate_row(part, share * piece + b) for b in range(piece)]
 
-    def tendency(part, share, b, value, rate_sum):
+    def tabulate(block, _):
+        through = [passing[block, rows(x), :] for x in range(layers)]
+        down, up = through[0], through[-1]
+        for x in range(layers):
+            back = layers - 1 - x
+            if x > 0:
+                down = through[x] * down
+                up = through[back] * up
+            from_below[block, rows(x), :] = (1.0 - through[x]) * down
+            from_above[block, rows(back), :] = (1.0 - through[back]) * up
+        return 0
+
+    def prepare(part, load):
+        def one_block(block, _):
+            value = load(block)
+            through = [passing[block, rows(x), :] for x in range(layers)]
+            emit = [emitted_of(value[x], block) for x in range(layers)]
+            downs, ups = [emit[0]], [emit[-1]]
+            for x in range(1, layers):
+                downs.append(through[x] * downs[-1] + emit[x])
+                ups.insert(0, through[layers - 1 - x] * ups[0] + emit[layers - 1 - x])
+            arrived = halo[part, block].astype(jnp.float32)
+            entering = jnp.where(cell == 0, inflow_ref[:, lanes(block)], arrived)
+            for x in range(layers):
+                taken = (1.0 - through[x]) * (downs[x] + ups[x] - 2.0 * emit[x])
+                upstream = entering if x == 0 else value[x - 1]
+                before_y = pltpu.roll(value[x], 1, 0)
+                after_y = pltpu.roll(value[x], NY - 1, 0)
+                cross = coef[2, rows(x), :]
+                carried = (
+                    -coef[1, rows(x), :] * (value[x] - upstream)
+                    - jnp.maximum(cross, 0.0) * (value[x] - before_y)
+                    - jnp.minimum(cross, 0.0) * (after_y - value[x])
+                )
+                if part:
+                    inside[block, rows(x), :] = taken
+                known[block, rows(x), :] = value[x] + time_step * (taken + carried - emit[x])
+            return 0
+
+        lax.fori_loop(0, blocks, one_block, 0, unroll=2)
+
+    def outside(part, share, b):
         block = share * piece + b
-        through = [passing[block, rows(x), :] for x in range(layers)]
-        emit = [emitted_of(value[x], block) for x in range(layers)]
         down, up = get(in_two, part, share, b)
-        downs, ups = [None] * layers, [None] * layers
-        for x in range(layers):
-            down = through[x] * down + emit[x]
-            downs[x] = down
-            back = layers - 1 - x
-            up = through[back] * up + emit[back]
-            ups[back] = up
-        arrived = halo[part, block].astype(jnp.float32)
-        entering = jnp.where(cell == 0, inflow_ref[:, lanes(block)], arrived)
-        gains, total = [], []
-        for x in range(layers):
-            gained = downs[x] + ups[x] - 2.0 * emit[x]
-            taken = (1.0 - through[x]) * gained
-            upstream = entering if x == 0 else value[x - 1]
-            before_y = pltpu.roll(value[x], 1, 0)
-            after_y = pltpu.roll(value[x], NY - 1, 0)
-            cross = coef[2, rows(x), :]
-            carried = (
-                -coef[1, rows(x), :] * (value[x] - upstream)
-                - jnp.maximum(cross, 0.0) * (value[x] - before_y)
-                - jnp.minimum(cross, 0.0) * (after_y - value[x])
-            )
-            gains.append(gained)
-            total.append(rate_sum[rows(x)] - emit[x] + taken + carried)
-        return gains, total
-
-    def exchange(part):
-        early = half // 2
+        return [
+            from_below[block, rows(x), :] * down + from_above[block, rows(x), :] * up
+            for x in range(layers)
+        ]
+
+    def exchange(part, load):
+        early = half // 2 if part else half // 4
         for index in range(early):
             forward(part, turn_of(index))
         enter(part)
-        for index in range(early, half):
+        for index in range(early, half - 1):
             forward(part, turn_of(index))
+        before_close(part)
+        prepare(part, load)
+        forward(part, turn_of(half - 1))
         all_gathered(part)
-        before_close(part)
 
     def arrived_two(part, share):
         @pl.when(share != pos)
         def _():
             two_copy(part, pos, share).wait_recv()
 
-    exchange(0)
+    lax.fori_loop(0, blocks, tabulate, 0)
+    exchange(0, load_start)
 
     def close_first(share, sums):
         arrived_two(0, share)
         values = []
         for b in range(piece):
             block = share * piece + b
-            value = load_start(block)
-            _, total = tendency(0, share, b, value, sums[b])
-            renewed = [value[x] + time_step * total[x] for x in range(layers)]
+            added = outside(0, share, b)
+            renewed = [
+                known[block, rows(x), :] + time_step * (sums[b][rows(x)] + added[x])
+                for x in range(layers)
+            ]
             for x in range(layers):
                 middle[block, rows(x), :] = renewed[x]
             lower(1, block, jnp.concatenate(renewed, axis=0))
@@ -528,18 +558,19 @@
     partner_copy(1, lev).start()
     start_halo(1)
     finish_transfers(0)
-    exchange(1)
+    exchange(1, load_middle)
     finish_transfers(1)
 
     def close_second(share, sums):
         arrived_two(1, share)
         for b in range(piece):
             block = share * piece + b
-            value = [middle[block, rows(x), :] for x in range(layers)]
-            gains, total = tendency(1, share, b, value, sums[b])
+            start = load_start(block)
+            added = outside(1, share, b)
             for x in range(layers):
-                gained_ref[rows(x), lanes(block)] = gains[x]
-                advanced_ref[rows(x), lanes(block)] = value[x] + time_step * total[x]
+                gained_ref[rows(x), lanes(block)] = 2.0 * (inside[block, rows(x), :] + added[x])
+                renewed = known[block, rows(x), :] + time_step * (sums[b][rows(x)] + added[x])
+                advanced_ref[rows(x), lanes(block)] = start[x] + renewed
 
     def own_first(index):
         return lax.rem(pos + index, half)
@@ -599,6 +630,10 @@
             pltpu.VMEM((4, cell_count, LANES), jnp.float32),
             pltpu.VMEM(layers_shape, jnp.float32),
             pltpu.VMEM(layers_shape, jnp.float32),
+            pltpu.VMEM(layers_shape, jnp.float32),
+            pltpu.VMEM(layers_shape, jnp.float32),
+            pltpu.VMEM(layers_shape, jnp.float32),
+            pltpu.VMEM(layers_shape, jnp.float32),
             pltpu.VMEM((groups * blocks, cell_count, LANES), jnp.bfloat16),
             pltpu.VMEM((groups * blocks, cell_count, LANES), jnp.bfloat16),
             pltpu.VMEM((2, blocks, NY, LANES), jnp.bfloat16),
@@ -781,8 +816,7 @@
                 inflow,
             )
         )
-        transmit = jnp.exp(-(absorber[:, None] * cross_section[None, :]))
-        return (0.5 * (populations + advanced), (1.0 - transmit) * gained)
+        return (0.5 * advanced, 0.5 * gained)
     first_rate, _ = tendency(
         populations,
         rate_blocks,

time: 28.3 us -> 27.8 us (0.982)
  Pallas kernels: 26.4 us -> 26 us
    pallas_call x1, Pallas kernels: 26.4 us -> 26 us  [fused(): pl.pallas_call(functools.partial(fused_kernel, strips, groups), out_shape...]
where the time goes in v4:
time: 27.8 us; the launch traced here: 27.7 us
  Pallas kernels  26 us (94%)
  other arithmetic  1.06 us (4%)
  between operations  0.64 us (2%)
    pallas_call x1, Pallas kernels, fused(): pl.pallas_call(functools.partial(fused_kernel, strips, groups), out_shape...  26 us
    mul x1, other arithmetic, local(): return (0.5 * advanced, 0.5 * gained)  1.06 us

profile of v4, /device:TPU:0, one launch (start us, length us, event | category | flops | bytes accessed | tf_op | source)
XLA Modules:
  0.0 27.7 jit_solution(13608850837440632852)
XLA Ops:
  0.6 26.0 %shard_map.113 = (f32[64,2048]{1,0:T(8,128)S(1)}, f32[64,2048]{1,0:T(8,128)S(1)}) custom-call(s32[6,16]{1,0:T(8,128)} %bitcast.9, f32[64,2048]{1,0:T(8,128)} %p_hbm.1, bf16[2,16,6,128,128]{4,3,2,1,0:T(8,128)(2,1)} %rates_hbm.1, s32[1,64]{1,0:T(1,128)} %bitcast.10, f32[1,64]{1,0:T(1,128)} %bitcast.11, f32[1,64]{1,0:T(1,128)} %bitcast.12, f32[1,64]{1,0:T(1,128)} %bitcast.13, ...), custom_call_target="tpu_custom_call" | custom-call | tf_op jit(solution)/shard_map/pallas_call | solution.py:622
  26.6 1.1 %broadcast_multiply_fusion = (f32[64,2048]{1,0:T(8,128)}, f32[64,2048]{1,0:T(8,128)}) fusion(f32[64,2048]{1,0:T(8,128)S(1)} %get-tuple-element.5, f32[64,2048]{1,0:T(8,128)S(1)} %get-tuple-element.4), kind=kLoop, calls=%fused_computation | loop fusion | flops 262144 | bytes 2097152 | tf_op jit(solution)/shard_map/mul | solution.py:819

commit v5 on v4

--- a/solution.py
+++ b/solution.py
@@ -329,12 +329,12 @@
     coef[0] = spread(absorber_ref[...])
     lax.fori_loop(0, half, summarize_start, 0)
     pl.semaphore_wait(barrier, greeted)
+    start_gather(0, turn_of(0))
     for step in range(1, strips):
         column_copy(step).start()
-    start_gather(0, turn_of(0))
+    start_gather(0, turn_of(1))
     for index in range(half):
         send_summary(0, turn_of(index))
-    start_gather(0, turn_of(1))
     for index in range(2, half):
         start_gather(0, turn_of(index))
     partner_copy(0, lev).start()
@@ -568,9 +568,9 @@
             start = load_start(block)
             added = outside(1, share, b)
             for x in range(layers):
-                gained_ref[rows(x), lanes(block)] = 2.0 * (inside[block, rows(x), :] + added[x])
+                gained_ref[rows(x), lanes(block)] = inside[block, rows(x), :] + added[x]
                 renewed = known[block, rows(x), :] + time_step * (sums[b][rows(x)] + added[x])
-                advanced_ref[rows(x), lanes(block)] = start[x] + renewed
+                advanced_ref[rows(x), lanes(block)] = 0.5 * (start[x] + renewed)
 
     def own_first(index):
         return lax.rem(pos + index, half)
@@ -580,6 +580,34 @@
         if index + 2 < half:
             ready.append(rates_of(1, own_first(index + 2)))
         close_second(own_first(index), ready[index])
+
+
+def deliver_kernel(first_ref, second_ref, first_hbm, second_hbm, sem):
+    count = sem.shape[1]
+    bite = first_ref.shape[0] // count
+    copies = [
+        pltpu.make_async_copy(
+            source.at[pl.ds(index * bite, bite)], into.at[pl.ds(index * bite, bite)], sem.at[which, index]
+        )
+        for index in range(count)
+        for which, (source, into) in enumerate(((first_ref, first_hbm), (second_ref, second_hbm)))
+    ]
+    for copy in copies:
+        copy.start()
+    for copy in copies:
+        copy.wait()
+
+
+def delivered(*values):
+    value = values[0]
+    count = 2 if value.shape[0] % (8 * 2) == 0 else 1
+    return pl.pallas_call(
+        deliver_kernel,
+        out_shape=[jax.ShapeDtypeStruct(value.shape, value.dtype)] * len(values),
+        in_specs=[pl.BlockSpec(memory_space=pltpu.VMEM)] * len(values),
+        out_specs=[pl.BlockSpec(memory_space=pltpu.HBM)] * len(values),
+        scratch_shapes=[pltpu.SemaphoreType.DMA((len(values), count))],
+    )(*[pltpu.with_memory_space_constraint(value, pltpu.VMEM) for value in values])
 
 
 def fused(
@@ -816,7 +844,7 @@
                 inflow,
             )
         )
-        return (0.5 * advanced, 0.5 * gained)
+        return delivered(advanced, gained)
     first_rate, _ = tendency(
         populations,
         rate_blocks,

time: 27.8 us -> 27.8 us (level)
  other arithmetic: 1.06 us -> 0 us
  Pallas kernels: 26 us -> 27 us
    mul x1 -> x0, other arithmetic: 1.06 us -> none  [local(): return (0.5 * advanced, 0.5 * gained)]
    pallas_call x0 -> x1, Pallas kernels: none -> 1 us  [delivered(): pl.pallas_call(deliver_kernel, out_shape=[jax.ShapeDtypeStruct(value.shap...]
where the time goes in v5:
time: 27.8 us; the launch traced here: 27.6 us
  Pallas kernels  27 us (97%)
  between operations  0.64 us (2%)
    pallas_call x1, Pallas kernels, fused(): pl.pallas_call(functools.partial(fused_kernel, strips, groups), out_shape...  26 us
    pallas_call x1, Pallas kernels, delivered(): pl.pallas_call(deliver_kernel, out_shape=[jax.ShapeDtypeStruct(value.shap...  1 us

profile of v5, /device:TPU:0, one launch (start us, length us, event | category | flops | bytes accessed | tf_op | source)
XLA Modules:
  0.0 27.6 jit_solution(11960877528996275289)
XLA Ops:
  0.6 26.0 %shard_map.113 = (f32[64,2048]{1,0:T(8,128)S(1)}, f32[64,2048]{1,0:T(8,128)S(1)}) custom-call(s32[6,16]{1,0:T(8,128)} %bitcast.9, f32[64,2048]{1,0:T(8,128)} %p_hbm.1, bf16[2,16,6,128,128]{4,3,2,1,0:T(8,128)(2,1)} %rates_hbm.1, s32[1,64]{1,0:T(1,128)} %bitcast.10, f32[1,64]{1,0:T(1,128)} %bitcast.11, f32[1,64]{1,0:T(1,128)} %bitcast.12, f32[1,64]{1,0:T(1,128)} %bitcast.13, ...), custom_call_target="tpu_custom_call" | custom-call | tf_op jit(solution)/shard_map/pallas_call | solution.py:650
  26.6 1.0 %shard_map.114 = (f32[64,2048]{1,0:T(8,128)}, f32[64,2048]{1,0:T(8,128)}) custom-call(f32[64,2048]{1,0:T(8,128)S(1)} %get-tuple-element.4.first_ref, f32[64,2048]{1,0:T(8,128)S(1)} %get-tuple-element.5.second_ref), custom_call_target="tpu_custom_call" | custom-call | tf_op jit(solution)/shard_map/pallas_call | solution.py:604
